TPU v7x, 128 devices: a whole 4x4x4 slice. The times are simulated.
128 devices in a mesh: row: 32 (over x, y, core), col: 4 (over z).
Axes of the slice: x: 4, y: 4, z: 4, core: 2. Of those that a mesh axis runs over, the one named last changes fastest.
Arguments:
- right_side: bfloat16 [65536, 4096], P(('row', 'col')), may hold values from -6 to 6
- factor: bfloat16 [65536, 2048], P(('row', 'col')), may hold values from -0.125 to 0.125
- diag_inverse: bfloat16 [2048, 512], P('col'), as said below
- tile_mask: int32 [128, 4], P(('row', 'col')), may hold values from 0 to 1, as said below
- window_rows: int32 [4], replicated, may hold values from 0 to 127, as said below
Outputs:
- solution: bfloat16 [2048, 4096], P('row', 'col')
- updated_rhs: bfloat16 [65536, 4096], P(('row', 'col'))
Inputs may be any that keep to these rules, and one draw needn't show every extreme that they name: `window_rows`: distinct stored panel numbers, panels 0 and 127 always among them; panel p is stored on device p // 1 of row+col, and the window panels lie on different devices. `tile_mask`: 0 or 1; in the row of window panel k the entries of columns k and beyond are 0. `diag_inverse`: each tile is lower triangular.
All inputs are finite; a program needn't handle non-finite values.
Results may differ from a plain program's by a relative error of at most 0.0056.
Values may be sent and summed in bfloat16 or wider, within the bound.
A program may use at most 128 MiB of HBM per device.

v0:
```python
import jax
import jax.numpy as jnp
from jax import lax
from jax.sharding import PartitionSpec as P

AXES = ("row", "col")
NT = (((1,), (1,)), ((), ()))


def dot_nt(a, b):
    return lax.dot_general(a, b, NT, preferred_element_type=jnp.float32)


def body(right_side, factor, diag_inverse, tile_mask, window_rows):
    panel = diag_inverse.shape[1]
    window = factor.shape[1] // panel
    columns = right_side.shape[1]
    ncol = lax.axis_size("col")
    nrow = lax.axis_size("row")
    ndev = nrow * ncol
    width = columns // ndev
    col_index = lax.axis_index("col")
    row_index = lax.axis_index("row")
    me = row_index * ncol + col_index
    present = jnp.repeat(tile_mask[0] > 0, panel)
    masked = jnp.where(present[None, :], factor, jnp.zeros_like(factor))
    pieces = lax.all_to_all(
        right_side.T.reshape(ndev, width, panel), AXES, split_axis=0, concat_axis=0, tiled=True
    )
    lower = []
    for k in range(1, window):
        mine = me == window_rows[k]
        for j in range(k):
            tile = masked[:, j * panel : (j + 1) * panel]
            lower.append(jnp.where(mine, tile, jnp.zeros_like(tile)))
    lower = lax.psum(jnp.stack(lower), AXES)
    inverses = lax.all_gather(diag_inverse, "col", axis=0, tiled=True).reshape(window, panel, panel)
    solved = []
    for k in range(window):
        residual = lax.dynamic_index_in_dim(pieces, window_rows[k], 0, keepdims=False).astype(
            jnp.float32
        )
        for j in range(k):
            residual = residual - dot_nt(solved[j], lower[k * (k - 1) // 2 + j])
        solved.append(dot_nt(residual.astype(jnp.bfloat16), inverses[k]).astype(jnp.bfloat16))
    whole = lax.all_gather(jnp.concatenate(solved, axis=1), AXES, axis=0, tiled=True)
    updated = (right_side.astype(jnp.float32) - dot_nt(masked, whole)).astype(jnp.bfloat16)
    block_rows = window * panel // nrow
    block_cols = columns // ncol
    solution = lax.dynamic_slice(
        whole, (col_index * block_cols, row_index * block_rows), (block_cols, block_rows)
    ).T
    return (solution, updated)


def solution(mesh):
    in_specs = (P(AXES, None), P(AXES, None), P("col", None), P(AXES, None), P())
    out_specs = (P("row", "col"), P(AXES, None))
    return jax.shard_map(body, mesh=mesh, in_specs=in_specs, out_specs=out_specs, check_vma=False)
```

profile of v0, /device:TPU:1, one launch (start us, length us, event | category | flops | bytes accessed | tf_op | source)
XLA Modules:
  0.0 338.8 jit_solution(7828299529200578639)
XLA Ops:
  8.0 0.0 all-gather.3.cloned.1.call-start
  8.0 0.7 all-gather.3.cloned.1.call-update
  8.7 6.4 %copy.8 = bf16[512,4096]{0,1:T(8,128)(2,1)} copy(bf16[512,4096]{1,0:T(8,128)(2,1)} %param.5) | data formatting | bytes 8388608 | tf_op args[0]
  15.1 12.0 %all-to-all-start = ((bf16[128,32,512]{2,1,0:T(8,128)(2,1)}), bf16[128,32,512]{2,1,0:T(8,128)(2,1)}, u32[]{:S(2)}, u32[]{:S(2)}) async-start(bf16[128,32,512]{2,1,0:T(8,128)(2,1)} %bitcast.72), calls=%async_computation | async-start | bytes 8388608 | tf_op jit(solution)/shard_map/all_to_all | solution.py:27
  27.1 0.0 all-reduce.2.cloned.1.call-start
  27.2 0.1 broadcast_bitcast_fusion
  27.3 0.6 fusion.16
  29.8 1.8 broadcast_select_fusion
  31.5 0.9 bitcast_dynamic-update-slice_fusion.4
  32.5 1.0 bitcast_dynamic-update-slice_fusion.3
  33.4 0.9 bitcast_dynamic-update-slice_fusion.2
  34.3 0.9 bitcast_dynamic-update-slice_fusion.1
  35.3 0.9 bitcast_dynamic-update-slice_fusion
  36.2 0.9 fusion.7
  37.1 0.0 all-reduce.2.cloned.1.call-update
  37.1 0.0 all-gather.5.cloned.1.call-start
  44.7 46.7 %all-gather.3.cloned.1.call-done = bf16[2048,512]{1,0:T(8,128)(2,1)} async-done(((bf16[512,512]{1,0:T(8,128)(2,1)}), bf16[2048,512]{1,0:T(8,128)(2,1)}) %all-gather.3.cloned.1.call-update) | async-done | bytes 2097168 | tf_op jit(solution)/shard_map/all_gather | solution.py:37
  91.4 0.0 all-to-all-done
  91.4 1.3 convolution_convert_fusion.3
  92.7 133.6 %all-reduce.2.cloned.1.call-done = bf16[6,512,512]{2,1,0:T(8,128)(2,1)} async-done(((bf16[6,512,512]{2,1,0:T(8,128)(2,1)}), bf16[6,512,512]{2,1,0:T(8,128)(2,1)}) %all-reduce.2.cloned.1.call-update) | async-done | bytes 3145744 | tf_op jit(solution)/shard_map/psum | solution.py:36
  226.3 1.3 convolution_subtract_fusion.4
  227.6 1.6 convolution_convert_fusion.2
  229.3 1.3 convolution_subtract_fusion.2
  230.6 1.6 convolution_convert_fusion.1
  232.2 1.3 convolution_subtract_fusion.1
  233.6 1.6 convolution_convert_fusion
  235.2 0.7 pad_maximum_fusion
  235.9 0.0 all-gather.5.cloned.1.call-update
  235.9 79.1 %all-gather.5.cloned.1.call-done = bf16[4096,2048]{1,0:T(8,128)(2,1)} async-done(((bf16[32,2048]{1,0:T(8,128)(2,1)}), bf16[4096,2048]{1,0:T(8,128)(2,1)}) %all-gather.5.cloned.1.call-update) | async-done | bytes 16777232 | tf_op jit(solution)/shard_map/all_gather | solution.py:46
  315.1 1.1 dynamic-slice_bitcast_fusion
  316.2 0.8 copy.9
  317.0 14.4 %subtract_convert_fusion = bf16[512,4096]{1,0:T(8,128)(2,1)} fusion(bf16[512,4096]{1,0:T(8,128)(2,1)} %param.5, bf16[512,2048]{1,0:T(8,128)(2,1)S(1)} %broadcast_select_fusion, bf16[4096,2048]{1,0:T(8,128)(2,1)} %all-gather.5.cloned.1.call-done), kind=kOutput, calls=%fused_computation | convolution fusion | flops 8596226048 | bytes 27262976 | tf_op jit(solution)/shard_map/dot_general | solution.py:11
  (6 shorter events, 0.0 us)
Async XLA Ops:
  8.0 83.4 %all-gather.3.cloned.1.call-start = ((), (), s32[]{:S(2)}) async-start(), calls=%async_computation.1 | async-start | bytes 2621440 | tf_op jit(solution)/shard_map/all_gather | solution.py:37
  15.1 12.0 %copy-start.1 = (s32[1,4]{1,0:T(1,128)S(1)}, s32[1,4]{1,0:T(1,128)}, u32[]{:S(2)}) copy-start(s32[1,4]{1,0:T(1,128)} %param.8) | copy-start | bytes 52
  15.1 12.1 %copy-start = (s32[4]{0:T(128)S(1)}, s32[4]{0:T(128)}, u32[]{:S(2)}) copy-start(s32[4]{0:T(128)} %param.9) | copy-start | bytes 52
  15.1 76.2 %all-to-all-start = ((bf16[128,32,512]{2,1,0:T(8,128)(2,1)}), bf16[128,32,512]{2,1,0:T(8,128)(2,1)}, u32[]{:S(2)}, u32[]{:S(2)}) async-start(bf16[128,32,512]{2,1,0:T(8,128)(2,1)} %bitcast.72), calls=%async_computation | async-start | bytes 8388608 | tf_op jit(solution)/shard_map/all_to_all | solution.py:27
  27.1 199.2 %all-reduce.2.cloned.1.call-start = ((), (), s32[]{:S(2)}) async-start(), calls=%async_computation.2 | async-start | bytes 6291456 | tf_op jit(solution)/shard_map/psum | solution.py:36
  37.1 278.0 %all-gather.5.cloned.1.call-start = ((), (), s32[]{:S(2)}) async-start(), calls=%async_computation.3 | async-start | bytes 16908288 | tf_op jit(solution)/shard_map/all_gather | solution.py:46
Sparse Core Ops, SparseCore 0:
  10.6 80.7 all-gather.2
Sparse Core Ops, SparseCore 1:
  37.2 189.1 all-reduce.1
  236.0 79.0 all-gather.4
where the time goes:
time: 339 us
  waiting for transfers between devices  260 us (77%)
  between operations  25 us (7%)
  matrix products  24.5 us (7%)
  starting transfers between devices  12.1 us (4%)
  local copies, waits for them, and re-layouts  9 us (3%)
  other arithmetic  8.01 us (2%)
    psum x1, waiting for transfers between devices, body(): lower = lax.psum(jnp.stack(lower), AXES)  134 us
    all_gather x1, waiting for transfers between devices, body(): lax.all_gather(jnp.concatenate(solved, axis=1), AXES, axis=0, tiled=True)  79.1 us
    all_gather x1, waiting for transfers between devices, body(): lax.all_gather(diag_inverse, 'col', axis=0, tiled=True)  46.7 us
    dot_general x8, matrix products, dot_nt(): return lax.dot_general(a, b, NT, preferred_element_type=jnp.float32)  24.5 us
    all_to_all x1, starting transfers between devices, body(): lax.all_to_all(right_side.T.reshape(ndev, width, panel), AXES, split_axis...  12 us
    unnamed x8, local copies, waits for them, and re-layouts  7.29 us
  transfers between devices with their start and end apart: 4, of which 3 were waited for; matrix products, arithmetic and copies ran while one was open for 5% of the time, Pallas kernels for 0%

commit v1 on v0

--- a/solution.py
+++ b/solution.py
@@ -5,6 +5,9 @@
 
 AXES = ("row", "col")
 NT = (((1,), (1,)), ((), ()))
+pack_set = lambda xx, axis_tag, dev_axis: jax.lax.psum(
+    jax.lax.psum(xx, axis_tag), axis_name=dev_axis
+)
 
 
 def dot_nt(a, b):
@@ -33,7 +36,7 @@
         for j in range(k):
             tile = masked[:, j * panel : (j + 1) * panel]
             lower.append(jnp.where(mine, tile, jnp.zeros_like(tile)))
-    lower = lax.psum(jnp.stack(lower), AXES)
+    lower = pack_set(jnp.stack(lower), "col", "row")
     inverses = lax.all_gather(diag_inverse, "col", axis=0, tiled=True).reshape(window, panel, panel)
     solved = []
     for k in range(window):

time: 339 us -> 402 us (1.19)
  waiting for transfers between devices: 260 us -> 323 us
    psum x1 -> x2, waiting for transfers between devices: 134 us -> 217 us  [the longest x1 111 us: jax.lax.psum(jax.lax.psum(xx, axis_tag), axis_name=dev_axis)]
    all_gather x1, waiting for transfers between devices: 46.7 us -> 25 us  [body(): lax.all_gather(diag_inverse, 'col', axis=0, tiled=True)]
  transfers between devices with their start and end apart: 4 -> 5, of which waited for: 3 -> 4; matrix products, arithmetic and copies ran while one was open for 5% -> 2% of each run, Pallas kernels for 0% -> 0%
where the time goes in v1:
time: 402 us; the launch traced here: 401 us
  waiting for transfers between devices  323 us (80%)
  matrix products  24.5 us (6%)
  between operations  23.1 us (6%)
  starting transfers between devices  12.1 us (3%)
  local copies, waits for them, and re-layouts  9.79 us (2%)
  other arithmetic  8.63 us (2%)
    psum x1, waiting for transfers between devices, jax.lax.psum(jax.lax.psum(xx, axis_tag), axis_name=dev_axis)  111 us
    psum x1, waiting for transfers between devices, jax.lax.psum(xx, axis_tag)  105 us
    all_gather x1, waiting for transfers between devices, body(): lax.all_gather(jnp.concatenate(solved, axis=1), AXES, axis=0, tiled=True)  80.7 us
    all_gather x1, waiting for transfers between devices, body(): lax.all_gather(diag_inverse, 'col', axis=0, tiled=True)  25 us
    dot_general x8, matrix products, dot_nt(): return lax.dot_general(a, b, NT, preferred_element_type=jnp.float32)  24.5 us
    all_to_all x1, starting transfers between devices, body(): lax.all_to_all(right_side.T.reshape(ndev, width, panel), AXES, split_axis...  12 us
  transfers between devices with their start and end apart: 5, of which 4 were waited for; matrix products, arithmetic and copies ran while one was open for 2% of the time, Pallas kernels for 0%

profile of v1, /device:TPU:1, one launch (start us, length us, event | category | flops | bytes accessed | tf_op | source)
XLA Modules:
  0.0 401.3 jit_solution(13019410600545195095)
XLA Ops:
  7.2 0.0 all-reduce.3.cloned.1.call-start
  7.2 1.4 fusion.16
  8.6 0.7 compare_bitcast_fusion
  9.3 0.1 broadcast_bitcast_fusion
  10.6 1.7 broadcast_select_fusion
  12.4 0.9 bitcast_dynamic-update-slice_fusion.4
  13.3 0.9 bitcast_dynamic-update-slice_fusion.3
  14.2 0.9 bitcast_dynamic-update-slice_fusion.2
  15.8 0.9 bitcast_dynamic-update-slice_fusion.1
  16.8 0.9 bitcast_dynamic-update-slice_fusion
  17.7 0.9 fusion.7
  18.6 0.0 all-gather.3.cloned.1.call-start
  18.6 0.7 all-gather.3.cloned.1.call-update
  19.3 6.4 %copy.8 = bf16[512,4096]{0,1:T(8,128)(2,1)} copy(bf16[512,4096]{1,0:T(8,128)(2,1)} %param.5) | data formatting | bytes 8388608 | tf_op args[0]
  25.7 12.0 %all-to-all-start = ((bf16[128,32,512]{2,1,0:T(8,128)(2,1)}), bf16[128,32,512]{2,1,0:T(8,128)(2,1)}, u32[]{:S(2)}, u32[]{:S(2)}) async-start(bf16[128,32,512]{2,1,0:T(8,128)(2,1)} %bitcast.72), calls=%async_computation | async-start | bytes 8388608 | tf_op jit(solution)/shard_map/all_to_all | solution.py:30
  37.7 0.0 all-reduce.5.cloned.1.call-start
  37.8 105.2 %all-reduce.3.cloned.1.call-done = bf16[6,512,512]{2,1,0:T(8,128)(2,1)} async-done(((bf16[6,512,512]{2,1,0:T(8,128)(2,1)}), bf16[6,512,512]{2,1,0:T(8,128)(2,1)}) %all-reduce.3.cloned.1.call-update) | async-done | bytes 3145744 | tf_op jit(solution)/shard_map/psum | solution.py:9
  143.0 0.0 all-gather.5.cloned.1.call-start
  150.4 25.0 %all-gather.3.cloned.1.call-done = bf16[2048,512]{1,0:T(8,128)(2,1)} async-done(((bf16[512,512]{1,0:T(8,128)(2,1)}), bf16[2048,512]{1,0:T(8,128)(2,1)}) %all-gather.3.cloned.1.call-update) | async-done | bytes 2097168 | tf_op jit(solution)/shard_map/all_gather | solution.py:40
  175.5 1.3 convolution_convert_fusion.3
  176.8 111.4 %all-reduce.5.cloned.1.call-done = bf16[6,512,512]{2,1,0:T(8,128)(2,1)} async-done(((bf16[6,512,512]{2,1,0:T(8,128)(2,1)}), bf16[6,512,512]{2,1,0:T(8,128)(2,1)}) %all-reduce.5.cloned.1.call-update) | async-done | bytes 3145744 | tf_op jit(solution)/shard_map/psum | solution.py:8
  288.1 1.3 convolution_subtract_fusion.4
  289.4 1.6 convolution_convert_fusion.2
  291.1 1.3 convolution_subtract_fusion.2
  292.4 1.6 convolution_convert_fusion.1
  294.0 1.3 convolution_subtract_fusion.1
  295.4 1.6 convolution_convert_fusion
  297.0 0.7 pad_maximum_fusion
  297.7 80.7 %all-gather.5.cloned.1.call-done = bf16[4096,2048]{1,0:T(8,128)(2,1)} async-done(((bf16[32,2048]{1,0:T(8,128)(2,1)}), bf16[4096,2048]{1,0:T(8,128)(2,1)}) %all-gather.5.cloned.1.call-update) | async-done | bytes 16777232 | tf_op jit(solution)/shard_map/all_gather | solution.py:49
  378.5 1.1 dynamic-slice_bitcast_fusion
  379.6 0.8 copy.9
  380.4 14.4 %subtract_convert_fusion = bf16[512,4096]{1,0:T(8,128)(2,1)} fusion(bf16[512,4096]{1,0:T(8,128)(2,1)} %param.5, bf16[512,2048]{1,0:T(8,128)(2,1)S(1)} %broadcast_select_fusion, bf16[4096,2048]{1,0:T(8,128)(2,1)} %all-gather.5.cloned.1.call-done), kind=kOutput, calls=%fused_computation | convolution fusion | flops 8596226048 | bytes 27262976 | tf_op jit(solution)/shard_map/dot_general | solution.py:14
  (5 shorter events, 0.1 us)
Async XLA Ops:
  7.2 135.8 %all-reduce.3.cloned.1.call-start = ((), (), s32[]{:S(2)}) async-start(), calls=%async_computation.2 | async-start | bytes 6291456 | tf_op jit(solution)/shard_map/psum | solution.py:9
  18.6 156.9 %all-gather.3.cloned.1.call-start = ((), (), s32[]{:S(2)}) async-start(), calls=%async_computation.1 | async-start | bytes 2621440 | tf_op jit(solution)/shard_map/all_gather | solution.py:40
  25.7 149.7 %all-to-all-start = ((bf16[128,32,512]{2,1,0:T(8,128)(2,1)}), bf16[128,32,512]{2,1,0:T(8,128)(2,1)}, u32[]{:S(2)}, u32[]{:S(2)}) async-start(bf16[128,32,512]{2,1,0:T(8,128)(2,1)} %bitcast.72), calls=%async_computation | async-start | bytes 8388608 | tf_op jit(solution)/shard_map/all_to_all | solution.py:30
  37.7 250.4 %all-reduce.5.cloned.1.call-start = ((), (), s32[]{:S(2)}) async-start(), calls=%async_computation.3 | async-start | bytes 6291456 | tf_op jit(solution)/shard_map/psum | solution.py:8
  143.0 235.5 %all-gather.5.cloned.1.call-start = ((), (), s32[]{:S(2)}) async-start(), calls=%async_computation.4 | async-start | bytes 16908288 | tf_op jit(solution)/shard_map/all_gather | solution.py:49
Sparse Core Ops, SparseCore 0:
  18.7 124.2 all-reduce.2
  144.7 30.7 all-gather.2
  178.8 109.2 all-reduce.4
  297.9 80.5 all-gather.4

commit v2 on v0

--- a/solution.py
+++ b/solution.py
@@ -5,6 +5,16 @@
 
 AXES = ("row", "col")
 NT = (((1,), (1,)), ((), ()))
+
+
+def play_the_scales(slab_in):
+    next_value = jnp.concatenate(
+        jax.lax.all_to_all(
+            jnp.stack([slab_in for _ in range(jax.lax.psum(1, "col"))], 0), "col", 0, 0
+        ),
+        0,
+    )
+    return next_value
 
 
 def dot_nt(a, b):
@@ -34,7 +44,7 @@
             tile = masked[:, j * panel : (j + 1) * panel]
             lower.append(jnp.where(mine, tile, jnp.zeros_like(tile)))
     lower = lax.psum(jnp.stack(lower), AXES)
-    inverses = lax.all_gather(diag_inverse, "col", axis=0, tiled=True).reshape(window, panel, panel)
+    inverses = play_the_scales(diag_inverse).reshape(window, panel, panel)
     solved = []
     for k in range(window):
         residual = lax.dynamic_index_in_dim(pieces, window_rows[k], 0, keepdims=False).astype(

time: 339 us -> 351 us (1.035)
  waiting for transfers between devices: 260 us -> 266 us
  local copies, waits for them, and re-layouts: 9 us -> 12.8 us
    all_gather x1 -> x0, waiting for transfers between devices: 46.7 us -> none  [body(): lax.all_gather(diag_inverse, 'col', axis=0, tiled=True)]
    all_to_all x1, waiting for transfers between devices: 0.01 us -> 37.3 us  [body(): lax.all_to_all(right_side.T.reshape(ndev, width, panel), AXES, split_axis...]
    all_to_all x0 -> x1, waiting for transfers between devices: none -> 19 us  [play_the_scales(): jax.lax.all_to_all(jnp.stack([slab_in for _ in range(jax.lax.psum(1, 'col...]
    all_to_all x0 -> x1, starting transfers between devices: none -> 5.86 us  [play_the_scales(): jax.lax.all_to_all(jnp.stack([slab_in for _ in range(jax.lax.psum(1, 'col...]
    unnamed x8 -> x10, local copies, waits for them, and re-layouts: 7.29 us -> 8.6 us
  transfers between devices with their start and end apart: 4 -> 4, of which waited for: 3 -> 4; matrix products, arithmetic and copies ran while one was open for 5% -> 4% of each run, Pallas kernels for 0% -> 0%
where the time goes in v2:
time: 351 us; the launch traced here: 350 us
  waiting for transfers between devices  266 us (76%)
  matrix products  24.5 us (7%)
  between operations  23.6 us (7%)
  starting transfers between devices  15.4 us (4%)
  local copies, waits for them, and re-layouts  12.8 us (4%)
  other arithmetic  7.98 us (2%)
    psum x1, waiting for transfers between devices, body(): lower = lax.psum(jnp.stack(lower), AXES)  130 us
    all_gather x1, waiting for transfers between devices, body(): lax.all_gather(jnp.concatenate(solved, axis=1), AXES, axis=0, tiled=True)  79.3 us
    all_to_all x1, waiting for transfers between devices, body(): lax.all_to_all(right_side.T.reshape(ndev, width, panel), AXES, split_axis...  37.3 us
    dot_general x8, matrix products, dot_nt(): return lax.dot_general(a, b, NT, preferred_element_type=jnp.float32)  24.5 us
    all_to_all x1, waiting for transfers between devices, play_the_scales(): jax.lax.all_to_all(jnp.stack([slab_in for _ in range(jax.lax.psum(1, 'col...  19 us
    all_to_all x1, starting transfers between devices, body(): lax.all_to_all(right_side.T.reshape(ndev, width, panel), AXES, split_axis...  9.45 us
    unnamed x10, local copies, waits for them, and re-layouts  8.6 us
  transfers between devices with their start and end apart: 4, of which 4 were waited for; matrix products, arithmetic and copies ran while one was open for 4% of the time, Pallas kernels for 0%

profile of v2, /device:TPU:1, one launch (start us, length us, event | category | flops | bytes accessed | tf_op | source)
XLA Modules:
  0.0 350.4 jit_solution(7928867839564084833)
XLA Ops:
  7.2 2.5 stack.28
  9.7 5.9 %all-to-all-start.1 = ((bf16[4,512,512]{2,1,0:T(8,128)(2,1)}), bf16[4,512,512]{2,1,0:T(8,128)(2,1)S(1)}, u32[]{:S(2)}, u32[]{:S(2)}) async-start(bf16[4,512,512]{2,1,0:T(8,128)(2,1)} %stack.28), calls=%async_computation.1 | async-start | bytes 4194304 | tf_op jit(solution)/shard_map/all_to_all | solution.py:12
  15.6 6.4 %copy.8 = bf16[512,4096]{0,1:T(8,128)(2,1)} copy(bf16[512,4096]{1,0:T(8,128)(2,1)} %param.5) | data formatting | bytes 8388608 | tf_op args[0]
  22.0 19.0 %all-to-all-done.1 = bf16[4,512,512]{2,1,0:T(8,128)(2,1)S(1)} async-done(((bf16[4,512,512]{2,1,0:T(8,128)(2,1)}), bf16[4,512,512]{2,1,0:T(8,128)(2,1)S(1)}, u32[]{:S(2)}, u32[]{:S(2)}) %all-to-all-start.1) | async-done | bytes 2097184 | tf_op jit(solution)/shard_map/all_to_all | solution.py:12
  41.0 1.3 copy-done
  42.3 9.4 %all-to-all-start = ((bf16[128,32,512]{2,1,0:T(8,128)(2,1)}), bf16[128,32,512]{2,1,0:T(8,128)(2,1)}, u32[]{:S(2)}, u32[]{:S(2)}) async-start(bf16[128,32,512]{2,1,0:T(8,128)(2,1)} %bitcast.84), calls=%async_computation | async-start | bytes 8388608 | tf_op jit(solution)/shard_map/all_to_all | solution.py:37
  51.8 0.0 all-reduce.2.cloned.1.call-start
  51.8 0.1 broadcast_bitcast_fusion
  51.9 0.6 fusion.12
  54.4 1.7 broadcast_select_fusion
  56.2 0.9 bitcast_dynamic-update-slice_fusion.4
  57.1 1.0 bitcast_dynamic-update-slice_fusion.3
  58.0 0.9 bitcast_dynamic-update-slice_fusion.2
  59.0 0.9 bitcast_dynamic-update-slice_fusion.1
  59.9 0.9 bitcast_dynamic-update-slice_fusion
  60.8 0.9 fusion.4
  61.7 0.0 all-reduce.2.cloned.1.call-update
  61.7 0.0 all-gather.2.cloned.1.call-start
  69.3 37.3 %all-to-all-done = bf16[128,32,512]{2,1,0:T(8,128)(2,1)} async-done(((bf16[128,32,512]{2,1,0:T(8,128)(2,1)}), bf16[128,32,512]{2,1,0:T(8,128)(2,1)}, u32[]{:S(2)}, u32[]{:S(2)}) %all-to-all-start) | async-done | bytes 4194336 | tf_op jit(solution)/shard_map/all_to_all | solution.py:37
  106.6 1.3 convolution_convert_fusion.3
  107.9 130.5 %all-reduce.2.cloned.1.call-done = bf16[6,512,512]{2,1,0:T(8,128)(2,1)} async-done(((bf16[6,512,512]{2,1,0:T(8,128)(2,1)}), bf16[6,512,512]{2,1,0:T(8,128)(2,1)}) %all-reduce.2.cloned.1.call-update) | async-done | bytes 3145744 | tf_op jit(solution)/shard_map/psum | solution.py:46
  238.4 1.3 convolution_subtract_fusion.4
  239.7 1.6 convolution_convert_fusion.2
  241.4 1.3 convolution_subtract_fusion.2
  242.7 1.6 convolution_convert_fusion.1
  244.3 1.3 convolution_subtract_fusion.1
  245.7 1.6 convolution_convert_fusion
  247.3 0.7 pad_maximum_fusion
  248.0 79.3 %all-gather.2.cloned.1.call-done = bf16[4096,2048]{1,0:T(8,128)(2,1)} async-done(((bf16[32,2048]{1,0:T(8,128)(2,1)}), bf16[4096,2048]{1,0:T(8,128)(2,1)}) %all-gather.2.cloned.1.call-update) | async-done | bytes 16777232 | tf_op jit(solution)/shard_map/all_gather | solution.py:56
  327.3 1.1 dynamic-slice_bitcast_fusion
  328.4 0.8 copy.9
  329.2 14.4 %subtract_convert_fusion = bf16[512,4096]{1,0:T(8,128)(2,1)} fusion(bf16[512,4096]{1,0:T(8,128)(2,1)} %param.5, bf16[512,2048]{1,0:T(8,128)(2,1)S(1)} %broadcast_select_fusion, bf16[4096,2048]{1,0:T(8,128)(2,1)} %all-gather.2.cloned.1.call-done), kind=kOutput, calls=%fused_computation | convolution fusion | flops 8596226048 | bytes 27262976 | tf_op jit(solution)/shard_map/dot_general | solution.py:21
  (8 shorter events, 0.0 us)
Async XLA Ops:
  9.7 31.3 %all-to-all-start.1 = ((bf16[4,512,512]{2,1,0:T(8,128)(2,1)}), bf16[4,512,512]{2,1,0:T(8,128)(2,1)S(1)}, u32[]{:S(2)}, u32[]{:S(2)}) async-start(bf16[4,512,512]{2,1,0:T(8,128)(2,1)} %stack.28), calls=%async_computation.1 | async-start | bytes 4194304 | tf_op jit(solution)/shard_map/all_to_all | solution.py:12
  41.0 1.3 copy-start
  41.0 10.8 %copy-start.2 = (s32[1,4]{1,0:T(1,128)S(1)}, s32[1,4]{1,0:T(1,128)}, u32[]{:S(2)}) copy-start(s32[1,4]{1,0:T(1,128)} %param.8) | copy-start | bytes 52
  41.0 10.9 %copy-start.1 = (s32[4]{0:T(128)S(1)}, s32[4]{0:T(128)}, u32[]{:S(2)}) copy-start(s32[4]{0:T(128)} %param.9) | copy-start | bytes 52
  42.3 64.3 %all-to-all-start = ((bf16[128,32,512]{2,1,0:T(8,128)(2,1)}), bf16[128,32,512]{2,1,0:T(8,128)(2,1)}, u32[]{:S(2)}, u32[]{:S(2)}) async-start(bf16[128,32,512]{2,1,0:T(8,128)(2,1)} %bitcast.84), calls=%async_computation | async-start | bytes 8388608 | tf_op jit(solution)/shard_map/all_to_all | solution.py:37
  51.8 186.7 %all-reduce.2.cloned.1.call-start = ((), (), s32[]{:S(2)}) async-start(), calls=%async_computation.2 | async-start | bytes 6291456 | tf_op jit(solution)/shard_map/psum | solution.py:46
  61.7 265.6 %all-gather.2.cloned.1.call-start = ((), (), s32[]{:S(2)}) async-start(), calls=%async_computation.3 | async-start | bytes 16908288 | tf_op jit(solution)/shard_map/all_gather | solution.py:56
Sparse Core Ops, SparseCore 0:
  61.9 176.5 all-reduce.1
  248.1 79.0 all-gather.1
